TPU v7x, 32 devices: a whole 2x2x4 slice. The times are simulated.
32 devices in a mesh: task: 16 (over z, x, core), tensor: 2 (over y).
Axes of the slice: x: 2, y: 2, z: 4, core: 2. Of those that a mesh axis runs over, the one named last changes fastest.
Arguments:
- inputs: bfloat16 [3072, 8192], P('task'), may hold values from -6 to 6
- queries: bfloat16 [3072, 4096], P('task', 'tensor'), may hold values from -6 to 6
- task_vectors: bfloat16 [8, 2, 8192, 1024], P(None, None, 'task', 'tensor'), may hold values from -0.0625 to 0.0625
- base_weights: bfloat16 [2, 8192, 1024], P(None, 'task', 'tensor'), may hold values from -0.0625 to 0.0625
- scale_exps: int32 [8, 2, 64, 8], P(None, None, 'task', 'tensor'), may hold values from -3 to 0
- coefs: float32 [8, 2], replicated, may hold values from 0.1 to 0.6
Outputs:
- attended: bfloat16 [3072, 4096], P('task', 'tensor')
- mean_entropy: float32 [], replicated
- coef_grad: float32 [8, 2], replicated
All inputs are finite; a program needn't handle non-finite values.
Results may differ from a plain program's by a relative error of at most 0.0087.
Values may be sent and summed in bfloat16 or wider, within the bound.
A program may use at most 128 MiB of HBM per device.

v0:
```python
import jax
import jax.numpy as jnp
from jax import lax
from jax.sharding import PartitionSpec as P

HEAD = 128
GROUP = 4
sharpen = 4.0
capping = 8.0
masked_value = -1e30


def dequantize(vectors, exponents):
    tasks, mats, rows, cols = vectors.shape
    row_blocks = exponents.shape[2]
    col_blocks = exponents.shape[3]
    factor = jnp.exp2(exponents.astype(jnp.float32))
    blocked = vectors.astype(jnp.float32).reshape(
        tasks, mats, row_blocks, rows // row_blocks, col_blocks, cols // col_blocks
    )
    blocked = blocked * factor[:, :, :, None, :, None]
    return blocked.reshape(tasks, mats, rows, cols)


def capped_logits(attended):
    return capping * jnp.tanh(sharpen * attended.astype(jnp.float32) / capping)


def entropy_grad(logits, expo, total, moment):
    average = moment / total
    entropy = jnp.log(total) - average
    slope = sharpen * (1.0 - (logits / capping) ** 2)
    d_out = (slope * (-(expo / total[:, None]) * (logits - average[:, None]))).astype(jnp.bfloat16)
    return (entropy, d_out)


def local(inputs, queries, task_vectors, base_weights, scale_exps, coefs):
    n_task = lax.axis_size("task")
    n_tensor = lax.axis_size("tensor")
    tok_count = inputs.shape[0]
    col_dev = task_vectors.shape[3]
    kv_local = col_dev // HEAD
    scaled = dequantize(task_vectors, scale_exps)
    merged = (
        base_weights.astype(jnp.float32) + jnp.sum(coefs[:, :, None, None] * scaled, axis=0)
    ).astype(jnp.bfloat16)
    projected = jnp.einsum(
        "td,mdc->mtc",
        inputs,
        lax.all_gather(merged, "task", axis=1, tiled=True),
        preferred_element_type=jnp.float32,
    )
    projected_b = projected.astype(jnp.bfloat16)
    keys_b = projected_b[0].reshape(tok_count, kv_local, HEAD)
    values_b = projected_b[1].reshape(tok_count, kv_local, HEAD)
    query_heads = queries.reshape(tok_count, kv_local, GROUP, HEAD)
    inverse = HEAD ** (-0.5)
    scores = (
        jnp.einsum("shrd,thd->hrst", query_heads, keys_b, preferred_element_type=jnp.float32)
        * inverse
    )
    position = jnp.arange(tok_count)
    causal = position[None, :] <= position[:, None]
    scores = jnp.where(causal, scores, masked_value)
    probs = jax.nn.softmax(scores, axis=-1)
    probs_b = probs.astype(jnp.bfloat16)
    outputs = jnp.einsum("hrst,thd->shrd", probs_b, values_b, preferred_element_type=jnp.float32)
    attended = outputs.astype(jnp.bfloat16).reshape(tok_count, kv_local * GROUP * HEAD)
    logits = capped_logits(attended)
    expo = jnp.exp(logits)
    total, moment = lax.psum((jnp.sum(expo, axis=1), jnp.sum(expo * logits, axis=1)), "tensor")
    entropy, d_out = entropy_grad(logits, expo, total, moment)
    entropy_part = jnp.sum(entropy) / n_tensor
    d_out_heads = d_out.reshape(tok_count, kv_local, GROUP, HEAD)
    d_probs = jnp.einsum(
        "shrd,thd->hrst", d_out_heads, values_b, preferred_element_type=jnp.float32
    )
    d_scores = (probs * (d_probs - jnp.sum(probs * d_probs, axis=-1, keepdims=True))).astype(
        jnp.bfloat16
    )
    d_keys = (
        jnp.einsum("hrst,shrd->thd", d_scores, query_heads, preferred_element_type=jnp.float32)
        * inverse
    )
    d_values = jnp.einsum(
        "hrst,shrd->thd", probs_b, d_out_heads, preferred_element_type=jnp.float32
    )
    d_kv = jnp.stack(
        [d_keys.reshape(tok_count, col_dev), d_values.reshape(tok_count, col_dev)]
    ).astype(jnp.bfloat16)
    input_rows = lax.all_to_all(inputs, "task", split_axis=1, concat_axis=0, tiled=True)
    weight_grads = jnp.einsum(
        "tr,mtc->mrc",
        input_rows,
        lax.all_gather(d_kv, "task", axis=1, tiled=True),
        preferred_element_type=jnp.float32,
    )
    coef_part = jnp.sum(weight_grads[None] * scaled, axis=(2, 3))
    entropy_sum, coef_grad = lax.psum((entropy_part, coef_part), ("task", "tensor"))
    mean_entropy = entropy_sum / (tok_count * n_task)
    return (attended, mean_entropy, coef_grad)


def solution(mesh):
    return jax.shard_map(
        local,
        mesh=mesh,
        in_specs=(
            P("task", None),
            P("task", "tensor"),
            P(None, None, "task", "tensor"),
            P(None, "task", "tensor"),
            P(None, None, "task", "tensor"),
            P(),
        ),
        out_specs=(P("task", "tensor"), P(), P()),
        check_vma=False,
    )
```

profile of v0, /device:TPU:0, one launch (start us, length us, event | category | flops | bytes accessed | tf_op | source)
XLA Modules:
  0.0 388.9 jit_solution(6853657786691911180)
XLA Ops:
  7.2 0.0 all-gather.3.cloned.1.call-start
  7.2 0.7 multiply_exponential_fusion
  7.9 0.1 copy.33
  8.1 6.1 %mul.78 = f32[8,2,4,128,4,128]{5,4,3,2,1,0:T(4,128)} broadcast(f32[8,2,4,4]{3,2,1,0:T(4,128)S(1)} %copy.33), dimensions={0,1,2,4} | broadcast | bytes 16778240 | tf_op jit(solution)/shard_map/mul | solution.py:21
  14.2 0.0 copy-start.7
  14.2 19.9 %mul.79 = f32[8,2,512,512]{3,2,1,0:T(8,128)} reshape(f32[8,2,4,128,4,128]{5,4,3,2,1,0:T(4,128)} %mul.78) | data formatting | bytes 33554432 | tf_op jit(solution)/shard_map/mul | solution.py:21
  34.1 0.0 copy-done.7
  34.1 0.1 copy.32
  34.2 0.0 copy-start.3
  34.2 9.7 %multiply_reduce_fusion.1 = f32[2,512,512]{2,1,0:T(8,128)S(1)} fusion(f32[8,2,512,512]{3,2,1,0:T(8,128)} %mul.79, bf16[8,2,512,512]{3,2,1,0:T(8,128)(2,1)} %param.8, f32[8,2]{1,0:T(8,128)S(1)} %copy.32), kind=kLoop, calls=%fused_computation.2 | loop fusion | flops 16252928 | bytes 27263040 | tf_op jit(solution)/shard_map/reduce_sum | solution.py:45
  43.9 0.0 copy-done.3
  43.9 0.0 copy-start
  43.9 1.4 add_convert_fusion
  45.2 0.0 all-gather.3.cloned.1.call-update
  45.3 0.0 all-gather.5.cloned.1.call-start
  45.3 3.0 reshape.37
  48.3 0.6 iota_compare_fusion
  48.9 125.7 %all-gather.3.cloned.1.call-done = bf16[2,8192,512]{2,1,0:T(8,128)(2,1)} async-done(((bf16[2,512,512]{2,1,0:T(8,128)(2,1)}), bf16[2,8192,512]{2,1,0:T(8,128)(2,1)}) %all-gather.3.cloned.1.call-update) | async-done | bytes 16777232 | tf_op jit(solution)/shard_map/all_gather | solution.py:50
  174.6 0.0 copy-done
  174.6 7.6 %fusion.26 = bf16[2,192,512]{2,1,0:T(8,128)(2,1)S(1)} fusion(bf16[2,8192,512]{2,1,0:T(8,128)(2,1)} %all-gather.3.cloned.1.call-done, bf16[192,8192]{1,0:T(8,128)(2,1)S(1)} %copy-done), kind=kOutput, calls=%fused_computation.38 | convolution fusion | flops 3221422080 | bytes 20316160 | tf_op jit(solution)/shard_map/td,mdc->mtc/dot_general | solution.py:47
  182.2 0.7 fusion.53
  182.9 1.0 reshape_squeeze.7
  183.9 0.7 reshape_squeeze.6
  184.6 0.0 copy-start.6
  184.6 1.7 fusion.43
  186.4 0.0 copy-done.6
  186.4 0.0 copy-start.5
  186.4 1.0 fusion.54
  187.4 0.0 copy-start.8
  187.4 0.0 copy-done.5
  187.4 1.9 exponential_reduce_fusion
  189.4 0.0 copy-done.8
  189.4 4.9 %all-reduce.1 = (f32[192]{0:T(256)S(1)}, f32[192]{0:T(256)S(1)}) all-reduce(f32[192]{0:T(256)S(1)} %get-tuple-element.7, f32[192]{0:T(256)S(1)} %get-tuple-element.6), channel_id=1, replica_groups=mesh['task'=16,'tensor'=2] {'tensor'}, use_global_device_ids=true, to_apply=%region_6.7 | all-reduce | flops 384 | bytes 3072 | tf_op jit(solution)/shard_map/psum | solution.py:71
  194.3 0.6 subtract_reduce_fusion
  194.9 0.0 copy-start.4
  194.9 0.0 copy-start.9
  194.9 3.6 fusion.1
  198.5 0.0 copy-done.4
  198.5 0.0 copy-done.9
  198.5 0.0 copy-start.2
  198.5 1.9 fusion.36
  200.5 0.0 copy-done.2
  200.5 0.9 fusion.37
  201.3 0.2 copy.41
  201.5 0.1 stack_reshape.8
  201.6 1.1 copy.42
  202.7 0.8 stack_reshape.9
  203.4 1.7 pad_maximum_fusion
  205.1 0.0 all-gather.5.cloned.1.call-update
  205.1 2.0 copy.74
  207.2 3.9 %all-to-all-start = ((bf16[192,16,512]{2,0,1:T(8,128)(2,1)}), bf16[192,16,512]{2,0,1:T(8,128)(2,1)S(1)}, u32[]{:S(2)}, u32[]{:S(2)}) async-start(bf16[192,16,512]{2,0,1:T(8,128)(2,1)} %bitcast.76), calls=%async_computation | async-start | bytes 6291456 | tf_op jit(solution)/shard_map/all_to_all | solution.py:91
  211.1 2.6 copy.38
  214.4 92.6 %all-to-all-done = bf16[192,16,512]{2,0,1:T(8,128)(2,1)S(1)} async-done(((bf16[192,16,512]{2,0,1:T(8,128)(2,1)}), bf16[192,16,512]{2,0,1:T(8,128)(2,1)S(1)}, u32[]{:S(2)}, u32[]{:S(2)}) %all-to-all-start) | async-done | bytes 3145760 | tf_op jit(solution)/shard_map/all_to_all | solution.py:91
  307.0 4.0 %all-gather.5.cloned.1.call-done = bf16[2,3072,512]{2,1,0:T(8,128)(2,1)} async-done(((bf16[2,192,512]{2,1,0:T(8,128)(2,1)}), bf16[2,3072,512]{2,1,0:T(8,128)(2,1)}) %all-gather.5.cloned.1.call-update) | async-done | bytes 6291472 | tf_op jit(solution)/shard_map/all_gather | solution.py:95
  311.0 7.6 %convolution_bitcast_fusion = f32[2,512,512]{1,2,0:T(8,128)} fusion(bf16[2,3072,512]{2,1,0:T(8,128)(2,1)} %all-gather.5.cloned.1.call-done, bf16[3072,512,1]{1,0,2:T(8,128)(2,1)S(1)} %bitcast.78), kind=kOutput, calls=%fused_computation.19 | convolution fusion | flops 3221225472 | bytes 11534336 | tf_op jit(solution)/shard_map/tr,mtc->mrc/dot_general | solution.py:92
  318.5 1.9 copy.44
  320.5 0.0 copy-start.1
  320.5 9.3 %multiply_reduce_fusion = f32[8,2]{1,0:T(8,128)S(1)} fusion(f32[8,2,512,512]{3,2,1,0:T(8,128)} %mul.79, bf16[8,2,512,512]{3,2,1,0:T(8,128)(2,1)} %param.8, f32[2,512,512]{2,1,0:T(8,128)S(1)} %copy.44), kind=kLoop, calls=%fused_computation.1 | loop fusion | flops 16777200 | bytes 27263040 | tf_op jit(solution)/shard_map/reduce_sum | solution.py:98
  329.8 0.0 copy-done.1
  329.8 1.5 reshape.38
  331.3 48.3 %all-reduce = (f32[]{:T(128)}, f32[8,2]{1,0:T(8,128)S(1)}) all-reduce(f32[]{:T(128)S(6)} %div.37, f32[8,2]{1,0:T(8,128)S(1)} %multiply_reduce_fusion), channel_id=1, replica_groups=mesh['task'=16,'tensor'=2] {'task','tensor'}, use_global_device_ids=true, to_apply=%region_8.9 | all-reduce | flops 17 | bytes 136 | tf_op jit(solution)/shard_map/psum | solution.py:99
  379.6 0.6 copy.45
Async XLA Ops:
  7.2 167.4 %all-gather.3.cloned.1.call-start = ((), (), s32[]{:S(2)}) async-start(), calls=%async_computation.1 | async-start | bytes 17825792 | tf_op jit(solution)/shard_map/all_gather | solution.py:50
  14.2 19.9 %copy-start.7 = (f32[8,2]{0,1:T(2,128)S(1)}, f32[8,2]{0,1:T(2,128)}, u32[]{:S(2)}) copy-start(f32[8,2]{0,1:T(2,128)} %param.11) | copy-start | bytes 196
  34.2 9.7 %copy-start.3 = (bf16[2,512,512]{2,1,0:T(8,128)(2,1)S(1)}, bf16[2,512,512]{2,1,0:T(8,128)(2,1)}, u32[]{:S(2)}) copy-start(bf16[2,512,512]{2,1,0:T(8,128)(2,1)} %param.9) | copy-start | bytes 3145732
  43.9 130.7 %copy-start = (bf16[192,8192]{1,0:T(8,128)(2,1)S(1)}, bf16[192,8192]{1,0:T(8,128)(2,1)}, u32[]{:S(2)}) copy-start(bf16[192,8192]{1,0:T(8,128)(2,1)} %param.6) | copy-start | bytes 9437188
  45.3 265.7 %all-gather.5.cloned.1.call-start = ((), (), s32[]{:S(2)}) async-start(), calls=%async_computation.2 | async-start | bytes 6684672 | tf_op jit(solution)/shard_map/all_gather | solution.py:95
  184.6 1.8 copy-start.6
  186.4 1.1 copy-start.5
  187.4 1.9 copy-start.8
  194.9 3.6 copy-start.4
  194.9 3.6 copy-start.9
  198.5 1.9 copy-start.2
  207.2 99.8 %all-to-all-start = ((bf16[192,16,512]{2,0,1:T(8,128)(2,1)}), bf16[192,16,512]{2,0,1:T(8,128)(2,1)S(1)}, u32[]{:S(2)}, u32[]{:S(2)}) async-start(bf16[192,16,512]{2,0,1:T(8,128)(2,1)} %bitcast.76), calls=%async_computation | async-start | bytes 6291456 | tf_op jit(solution)/shard_map/all_to_all | solution.py:91
  320.5 9.3 %copy-start.1 = (bf16[192,4,4,128]{3,2,1,0:T(4,128)(2,1)S(1)}, bf16[192,4,4,128]{3,2,1,0:T(4,128)(2,1)}, u32[]{:S(2)}) copy-start(bf16[192,4,4,128]{3,2,1,0:T(4,128)(2,1)} %copy.38) | copy-start | bytes 2359300
Sparse Core Ops, SparseCore 0:
  45.4 129.1 all-gather.2
  205.3 105.6 all-gather.4
where the time goes:
time: 390 us; the launch traced here: 389 us
  waiting for transfers between devices  222 us (57%)
  blocking collectives  53.2 us (14%)
  local copies, waits for them, and re-layouts  42.4 us (11%)
  matrix products  25.2 us (6%)
  other arithmetic  25.1 us (6%)
  between operations  16.6 us (4%)
  starting transfers between devices  4 us (1%)
    all_gather x1, waiting for transfers between devices, local(): lax.all_gather(merged, 'task', axis=1, tiled=True)  126 us
    all_to_all x1, waiting for transfers between devices, local(): lax.all_to_all(inputs, 'task', split_axis=1, concat_axis=0, tiled=True)  92.6 us
    psum x1, blocking collectives, local(): lax.psum((entropy_part, coef_part), ('task', 'tensor'))  48.3 us
    mul x2, local copies, waits for them, and re-layouts, dequantize(): blocked = blocked * factor[:, :, :, None, :, None]  26 us
    reduce_sum x1, other arithmetic, local(): jnp.sum(coefs[:, :, None, None] * scaled, axis=0)  9.68 us
    reduce_sum x1, other arithmetic, local(): coef_part = jnp.sum(weight_grads[None] * scaled, axis=(2, 3))  9.33 us
  transfers between devices with their start and end apart: 3, of which 3 were waited for; matrix products, arithmetic and copies ran while one was open for 2% of the time, Pallas kernels for 0%

commit v1 on v0

--- a/solution.py
+++ b/solution.py
@@ -8,6 +8,22 @@
 sharpen = 4.0
 capping = 8.0
 masked_value = -1e30
+
+
+def ring_product(x, axis, dim, contribution):
+    devices, index, span = (lax.axis_size(axis), lax.axis_index(axis), x.shape[dim])
+    ahead = [(i, (i + 1) % devices) for i in range(devices)]
+    left = [(i, (i - 1) % devices) for i in range(devices)]
+    middle = devices // 2
+    from_left = from_right = x
+    subtotal = contribution(x, index * span)
+    for step in range(1, middle + 1):
+        from_left = lax.ppermute(from_left, axis, ahead)
+        if step < devices - middle:
+            from_right = lax.ppermute(from_right, axis, left)
+            subtotal = subtotal + contribution(from_right, (index + step) % devices * span)
+        subtotal = subtotal + contribution(from_left, (index - step) % devices * span)
+    return subtotal
 
 
 def dequantize(vectors, exponents):
@@ -44,11 +60,16 @@
     merged = (
         base_weights.astype(jnp.float32) + jnp.sum(coefs[:, :, None, None] * scaled, axis=0)
     ).astype(jnp.bfloat16)
-    projected = jnp.einsum(
-        "td,mdc->mtc",
-        inputs,
-        lax.all_gather(merged, "task", axis=1, tiled=True),
-        preferred_element_type=jnp.float32,
+    projected = ring_product(
+        merged,
+        "task",
+        1,
+        lambda part, start: jnp.einsum(
+            "td,mdc->mtc",
+            lax.dynamic_slice_in_dim(inputs, start, part.shape[1], axis=1),
+            part,
+            preferred_element_type=jnp.float32,
+        ),
     )
     projected_b = projected.astype(jnp.bfloat16)
     keys_b = projected_b[0].reshape(tok_count, kv_local, HEAD)

time: 390 us -> 447 us (1.15)
  starting transfers between devices: 4 us -> 152 us
  waiting for transfers between devices: 222 us -> 123 us
  matrix products: 25.2 us -> 31.2 us
    ppermute x0 -> x15, starting transfers between devices: none -> 134 us  [the longest x8 128 us: ring_product(): from_left = lax.ppermute(from_left, axis, ahead)]
    all_gather x1 -> x0, waiting for transfers between devices: 126 us -> none  [local(): lax.all_gather(merged, 'task', axis=1, tiled=True)]
    ppermute x0 -> x15, waiting for transfers between devices: none -> 27.3 us  [the longest x8 27.3 us: ring_product(): from_left = lax.ppermute(from_left, axis, ahead)]
    all_to_all x1, starting transfers between devices: 3.92 us -> 18.5 us  [local(): lax.all_to_all(inputs, 'task', split_axis=1, concat_axis=0, tiled=True)]
    dot_general x1 -> x16, matrix products: 7.62 us -> 13.6 us  [local(): jnp.einsum('td,mdc->mtc', lax.dynamic_slice_in_dim(inputs, start, part.sh...]
  transfers between devices with their start and end apart: 3 -> 17, of which waited for: 3 -> 7; matrix products, arithmetic and copies ran while one was open for 2% -> 5% of each run, Pallas kernels for 0% -> 0%
where the time goes in v1:
time: 447 us; the launch traced here: 446 us
  starting transfers between devices  152 us (34%)
  waiting for transfers between devices  123 us (28%)
  blocking collectives  54.3 us (12%)
  local copies, waits for them, and re-layouts  44 us (10%)
  matrix products  31.2 us (7%)
  other arithmetic  24.1 us (5%)
  between operations  16.9 us (4%)
    ppermute x8, starting transfers between devices, ring_product(): from_left = lax.ppermute(from_left, axis, ahead)  128 us
    all_to_all x1, waiting for transfers between devices, local(): lax.all_to_all(inputs, 'task', split_axis=1, concat_axis=0, tiled=True)  92.3 us
    psum x1, blocking collectives, local(): lax.psum((entropy_part, coef_part), ('task', 'tensor'))  49.4 us
    ppermute x8, waiting for transfers between devices, ring_product(): from_left = lax.ppermute(from_left, axis, ahead)  27.3 us
    mul x2, local copies, waits for them, and re-layouts, dequantize(): blocked = blocked * factor[:, :, :, None, :, None]  26 us
    all_to_all x1, starting transfers between devices, local(): lax.all_to_all(inputs, 'task', split_axis=1, concat_axis=0, tiled=True)  18.5 us
    dot_general x16, matrix products, local(): jnp.einsum('td,mdc->mtc', lax.dynamic_slice_in_dim(inputs, start, part.sh...  13.6 us
    reduce_sum x1, other arithmetic, local(): jnp.sum(coefs[:, :, None, None] * scaled, axis=0)  9.68 us
  transfers between devices with their start and end apart: 17, of which 7 were waited for; matrix products, arithmetic and copies ran while one was open for 5% of the time, Pallas kernels for 0%

profile of v1, /device:TPU:0, one launch (start us, length us, event | category | flops | bytes accessed | tf_op | source)
XLA Modules:
  0.0 445.6 jit_solution(12020276156993527507)
XLA Ops:
  7.2 0.7 multiply_exponential_fusion
  8.1 6.1 %mul.126 = f32[8,2,4,128,4,128]{5,4,3,2,1,0:T(4,128)} broadcast(f32[8,2,4,4]{3,2,1,0:T(4,128)S(1)} %copy.33), dimensions={0,1,2,4} | broadcast | bytes 16778240 | tf_op jit(solution)/shard_map/mul | solution.py:37
  14.2 19.9 %mul.127 = f32[8,2,512,512]{3,2,1,0:T(8,128)} reshape(f32[8,2,4,128,4,128]{5,4,3,2,1,0:T(4,128)} %mul.126) | data formatting | bytes 33554432 | tf_op jit(solution)/shard_map/mul | solution.py:37
  34.2 9.7 %multiply_reduce_fusion.1 = f32[2,512,512]{2,1,0:T(8,128)S(1)} fusion(f32[8,2,512,512]{3,2,1,0:T(8,128)} %mul.127, bf16[8,2,512,512]{3,2,1,0:T(8,128)(2,1)} %param.8, f32[8,2]{1,0:T(8,128)S(1)} %copy.32), kind=kLoop, calls=%fused_computation.2 | loop fusion | flops 16252928 | bytes 27263040 | tf_op jit(solution)/shard_map/reduce_sum | solution.py:61
  43.9 0.4 add_convert_fusion
  44.3 0.5 collective-permute-start.1
  44.8 0.5 copy-done.1
  45.3 5.4 %collective-permute-start = (bf16[2,512,512]{2,1,0:T(8,128)(2,1)S(1)}, bf16[2,512,512]{2,1,0:T(8,128)(2,1)S(1)}, u32[]{:S(2)}, u32[]{:S(2)}) collective-permute-start(bf16[2,512,512]{2,1,0:T(8,128)(2,1)S(1)} %add_convert_fusion), channel_id=1, source_target_pairs={{0,30},{2,0},{4,2},{6,4},{8,6},{10,8},{12,10},{14,12},{16,14},{18,... | collective-permute-start | bytes 3145736 | tf_op jit(solution)/shard_map/ppermute | solution.py:23
  50.7 11.6 %collective-permute-done.1 = bf16[2,512,512]{2,1,0:T(8,128)(2,1)S(1)} collective-permute-done((bf16[2,512,512]{2,1,0:T(8,128)(2,1)S(1)}, bf16[2,512,512]{2,1,0:T(8,128)(2,1)S(1)}, u32[]{:S(2)}, u32[]{:S(2)}) %collective-permute-start.1) | collective-permute-done | bytes 1048608 | tf_op jit(solution)/shard_map/ppermute | solution.py:21
  62.4 8.0 %collective-permute-start.3 = (bf16[2,512,512]{2,1,0:T(8,128)(2,1)S(1)}, bf16[2,512,512]{2,1,0:T(8,128)(2,1)S(1)}, u32[]{:S(2)}, u32[]{:S(2)}) collective-permute-start(bf16[2,512,512]{2,1,0:T(8,128)(2,1)S(1)} %collective-permute-done.1), channel_id=1, source_target_pairs={{0,2},{2,4},{4,6},{6,8},{8,10},{10,12},{12,14},{14,16},{16,18},{18... | collective-permute-start | bytes 3145736 | tf_op jit(solution)/shard_map/ppermute | solution.py:21
  70.5 8.9 %collective-permute-done.3 = bf16[2,512,512]{2,1,0:T(8,128)(2,1)S(1)} collective-permute-done((bf16[2,512,512]{2,1,0:T(8,128)(2,1)S(1)}, bf16[2,512,512]{2,1,0:T(8,128)(2,1)S(1)}, u32[]{:S(2)}, u32[]{:S(2)}) %collective-permute-start.3) | collective-permute-done | bytes 1048608 | tf_op jit(solution)/shard_map/ppermute | solution.py:21
  79.4 15.8 %collective-permute-start.5 = (bf16[2,512,512]{2,1,0:T(8,128)(2,1)S(1)}, bf16[2,512,512]{2,1,0:T(8,128)(2,1)S(1)}, u32[]{:S(2)}, u32[]{:S(2)}) collective-permute-start(bf16[2,512,512]{2,1,0:T(8,128)(2,1)S(1)} %collective-permute-done.3), channel_id=1, source_target_pairs={{0,2},{2,4},{4,6},{6,8},{8,10},{10,12},{12,14},{14,16},{16,18},{18... | collective-permute-start | bytes 3145736 | tf_op jit(solution)/shard_map/ppermute | solution.py:21
  95.2 3.5 collective-permute-done.5
  98.7 1.1 copy-done.9
  99.8 21.1 %collective-permute-start.7 = (bf16[2,512,512]{2,1,0:T(8,128)(2,1)S(1)}, bf16[2,512,512]{2,1,0:T(8,128)(2,1)}, u32[]{:S(2)}, u32[]{:S(2)}) collective-permute-start(bf16[2,512,512]{2,1,0:T(8,128)(2,1)S(1)} %collective-permute-done.5), channel_id=1, source_target_pairs={{0,2},{2,4},{4,6},{6,8},{8,10},{10,12},{12,14},{14,16},{16,18},{18... | collective-permute-start | bytes 3145736 | tf_op jit(solution)/shard_map/ppermute | solution.py:21
  120.9 2.4 collective-permute-done.7
  123.4 22.5 %collective-permute-start.9 = (bf16[2,512,512]{2,1,0:T(8,128)(2,1)}, bf16[2,512,512]{2,1,0:T(8,128)(2,1)}, u32[]{:S(2)}, u32[]{:S(2)}) collective-permute-start(bf16[2,512,512]{2,1,0:T(8,128)(2,1)} %collective-permute-done.7), channel_id=1, source_target_pairs={{0,2},{2,4},{4,6},{6,8},{8,10},{10,12},{12,14},{14,16},{16,18},{18... | collective-permute-start | bytes 3145736 | tf_op jit(solution)/shard_map/ppermute | solution.py:21
  145.8 3.0 reshape.37
  148.8 0.6 iota_compare_fusion
  149.5 1.6 fusion.67
  151.1 1.8 convolution_add_fusion.8
  152.9 0.4 convolution_add_fusion.7
  153.3 18.4 %collective-permute-start.11 = (bf16[2,512,512]{2,1,0:T(8,128)(2,1)}, bf16[2,512,512]{2,1,0:T(8,128)(2,1)S(1)}, u32[]{:S(2)}, u32[]{:S(2)}) collective-permute-start(bf16[2,512,512]{2,1,0:T(8,128)(2,1)} %collective-permute-done.9), channel_id=1, source_target_pairs={{0,2},{2,4},{4,6},{6,8},{8,10},{10,12},{12,14},{14,16},{16,18},{18... | collective-permute-start | bytes 3145736 | tf_op jit(solution)/shard_map/ppermute | solution.py:21
  171.7 0.4 fusion.62
  172.1 0.4 fusion.23
  172.5 0.4 fusion.59
  173.0 1.6 fusion.22
  174.6 21.8 %collective-permute-start.13 = (bf16[2,512,512]{2,1,0:T(8,128)(2,1)S(1)}, bf16[2,512,512]{2,1,0:T(8,128)(2,1)S(1)}, u32[]{:S(2)}, u32[]{:S(2)}) collective-permute-start(bf16[2,512,512]{2,1,0:T(8,128)(2,1)S(1)} %collective-permute-done.11), channel_id=1, source_target_pairs={{0,2},{2,4},{4,6},{6,8},{8,10},{10,12},{12,14},{14,16},{16,18},{18... | collective-permute-start | bytes 3145736 | tf_op jit(solution)/shard_map/ppermute | solution.py:21
  196.4 1.6 fusion.56
  198.0 1.6 fusion.21
  199.6 1.6 fusion.53
  201.3 0.4 fusion.20
  201.7 20.0 %collective-permute-start.14 = (bf16[2,512,512]{2,1,0:T(8,128)(2,1)S(1)}, bf16[2,512,512]{2,1,0:T(8,128)(2,1)S(1)}, u32[]{:S(2)}, u32[]{:S(2)}) collective-permute-start(bf16[2,512,512]{2,1,0:T(8,128)(2,1)S(1)} %collective-permute-done.13), channel_id=1, source_target_pairs={{0,2},{2,4},{4,6},{6,8},{8,10},{10,12},{12,14},{14,16},{16,18},{18... | collective-permute-start | bytes 3145736 | tf_op jit(solution)/shard_map/ppermute | solution.py:21
  221.7 0.4 fusion.50
  222.1 0.4 fusion.19
  222.5 0.4 fusion.47
  222.9 0.4 fusion.18
  223.3 0.8 collective-permute-done.14
  224.0 0.4 fusion.25
  224.4 0.7 fusion.108
  225.1 1.0 reshape_squeeze.7
  226.1 0.7 reshape_squeeze.6
  226.8 1.7 fusion.43
  228.6 1.0 fusion.109
  229.6 1.9 exponential_reduce_fusion
  231.6 4.9 %all-reduce.1 = (f32[192]{0:T(256)S(1)}, f32[192]{0:T(256)S(1)}) all-reduce(f32[192]{0:T(256)S(1)} %get-tuple-element.7, f32[192]{0:T(256)S(1)} %get-tuple-element.6), channel_id=1, replica_groups=mesh['task'=16,'tensor'=2] {'tensor'}, use_global_device_ids=true, to_apply=%region_6.7 | all-reduce | flops 384 | bytes 3072 | tf_op jit(solution)/shard_map/psum | solution.py:92
  236.5 0.6 subtract_reduce_fusion
  237.1 3.6 fusion.1
  240.7 1.9 fusion.36
  242.7 0.9 fusion.37
  243.8 1.1 copy.42
  244.9 0.8 stack_reshape.9
  245.6 1.7 pad_maximum_fusion
  247.4 2.0 copy.74
  249.4 18.5 %all-to-all-start = ((bf16[192,16,512]{2,0,1:T(8,128)(2,1)}), bf16[192,16,512]{2,0,1:T(8,128)(2,1)S(1)}, u32[]{:S(2)}, u32[]{:S(2)}) async-start(bf16[192,16,512]{2,0,1:T(8,128)(2,1)} %bitcast.132), calls=%async_computation | async-start | bytes 6291456 | tf_op jit(solution)/shard_map/all_to_all | solution.py:112
  267.9 2.7 copy.38
  271.2 92.3 %all-to-all-done = bf16[192,16,512]{2,0,1:T(8,128)(2,1)S(1)} async-done(((bf16[192,16,512]{2,0,1:T(8,128)(2,1)}), bf16[192,16,512]{2,0,1:T(8,128)(2,1)S(1)}, u32[]{:S(2)}, u32[]{:S(2)}) %all-to-all-start) | async-done | bytes 3145760 | tf_op jit(solution)/shard_map/all_to_all | solution.py:112
  363.5 3.1 all-gather.2.cloned.1.call-done
  366.6 7.6 %convolution_bitcast_fusion = f32[2,512,512]{1,2,0:T(8,128)} fusion(bf16[2,3072,512]{2,1,0:T(8,128)(2,1)} %all-gather.2.cloned.1.call-done, bf16[3072,512,1]{1,0,2:T(8,128)(2,1)S(1)} %bitcast.134), kind=kOutput, calls=%fused_computation.17 | convolution fusion | flops 3221225472 | bytes 11534336 | tf_op jit(solution)/shard_map/tr,mtc->mrc/dot_general | solution.py:113
  374.2 1.9 copy.44
  376.1 9.3 %multiply_reduce_fusion = f32[8,2]{1,0:T(8,128)S(1)} fusion(f32[8,2,512,512]{3,2,1,0:T(8,128)} %mul.127, bf16[8,2,512,512]{3,2,1,0:T(8,128)(2,1)} %param.8, f32[2,512,512]{2,1,0:T(8,128)S(1)} %copy.44), kind=kLoop, calls=%fused_computation.1 | loop fusion | flops 16777200 | bytes 27263040 | tf_op jit(solution)/shard_map/reduce_sum | solution.py:119
  385.4 1.5 reshape.38
  386.9 49.4 %all-reduce = (f32[]{:T(128)}, f32[8,2]{1,0:T(8,128)S(1)}) all-reduce(f32[]{:T(128)S(6)} %div.37, f32[8,2]{1,0:T(8,128)S(1)} %multiply_reduce_fusion), channel_id=1, replica_groups=mesh['task'=16,'tensor'=2] {'task','tensor'}, use_global_device_ids=true, to_apply=%region_8.9 | all-reduce | flops 17 | bytes 136 | tf_op jit(solution)/shard_map/psum | solution.py:120
  436.3 0.6 copy.45
  (60 shorter events, 0.9 us)
Async XLA Ops:
  7.2 359.4 %all-gather.2.cloned.1.call-start = ((), (), s32[]{:S(2)}) async-start(), calls=%async_computation.1 | async-start | bytes 6684672 | tf_op jit(solution)/shard_map/all_gather | solution.py:116
  14.2 19.9 %copy-start.17 = (f32[8,2]{0,1:T(2,128)S(1)}, f32[8,2]{0,1:T(2,128)}, u32[]{:S(2)}) copy-start(f32[8,2]{0,1:T(2,128)} %param.11) | copy-start | bytes 196
  34.2 9.7 %copy-start.11 = (bf16[2,512,512]{2,1,0:T(8,128)(2,1)S(1)}, bf16[2,512,512]{2,1,0:T(8,128)(2,1)}, u32[]{:S(2)}) copy-start(bf16[2,512,512]{2,1,0:T(8,128)(2,1)} %param.9) | copy-start | bytes 3145732
  43.9 105.6 %copy-start = (bf16[192,8192]{1,0:T(8,128)(2,1)S(1)}, bf16[192,8192]{1,0:T(8,128)(2,1)}, u32[]{:S(2)}) copy-start(bf16[192,8192]{1,0:T(8,128)(2,1)} %param.6) | copy-start | bytes 9437188
  44.3 1.0 copy-start.1
  44.3 18.1 %collective-permute-start.1 = (bf16[2,512,512]{2,1,0:T(8,128)(2,1)S(1)}, bf16[2,512,512]{2,1,0:T(8,128)(2,1)S(1)}, u32[]{:S(2)}, u32[]{:S(2)}) collective-permute-start(bf16[2,512,512]{2,1,0:T(8,128)(2,1)S(1)} %add_convert_fusion), channel_id=1, source_target_pairs={{0,2},{2,4},{4,6},{6,8},{8,10},{10,12},{12,14},{14,16},{16,18},{18... | collective-permute-start | bytes 3145736 | tf_op jit(solution)/shard_map/ppermute | solution.py:21
  45.3 25.1 %collective-permute-start = (bf16[2,512,512]{2,1,0:T(8,128)(2,1)S(1)}, bf16[2,512,512]{2,1,0:T(8,128)(2,1)S(1)}, u32[]{:S(2)}, u32[]{:S(2)}) collective-permute-start(bf16[2,512,512]{2,1,0:T(8,128)(2,1)S(1)} %add_convert_fusion), channel_id=1, source_target_pairs={{0,30},{2,0},{4,2},{6,4},{8,6},{10,8},{12,10},{14,12},{16,14},{18,... | collective-permute-start | bytes 3145736 | tf_op jit(solution)/shard_map/ppermute | solution.py:23
  62.4 8.0 %copy-start.4 = (bf16[2,512,512]{2,1,0:T(8,128)(2,1)}, bf16[2,512,512]{2,1,0:T(8,128)(2,1)S(1)}, u32[]{:S(2)}) copy-start(bf16[2,512,512]{2,1,0:T(8,128)(2,1)S(1)} %collective-permute-done.1) | copy-start | bytes 3145732
  62.4 17.0 %collective-permute-start.3 = (bf16[2,512,512]{2,1,0:T(8,128)(2,1)S(1)}, bf16[2,512,512]{2,1,0:T(8,128)(2,1)S(1)}, u32[]{:S(2)}, u32[]{:S(2)}) collective-permute-start(bf16[2,512,512]{2,1,0:T(8,128)(2,1)S(1)} %collective-permute-done.1), channel_id=1, source_target_pairs={{0,2},{2,4},{4,6},{6,8},{8,10},{10,12},{12,14},{14,16},{16,18},{18... | collective-permute-start | bytes 3145736 | tf_op jit(solution)/shard_map/ppermute | solution.py:21
  70.4 9.0 %copy-start.6 = (bf16[2,512,512]{2,1,0:T(8,128)(2,1)}, bf16[2,512,512]{2,1,0:T(8,128)(2,1)S(1)}, u32[]{:S(2)}) copy-start(bf16[2,512,512]{2,1,0:T(8,128)(2,1)S(1)} %collective-permute-done) | copy-start | bytes 3145732
  70.4 24.7 %collective-permute-start.2 = (bf16[2,512,512]{2,1,0:T(8,128)(2,1)S(1)}, bf16[2,512,512]{2,1,0:T(8,128)(2,1)S(1)}, u32[]{:S(2)}, u32[]{:S(2)}) collective-permute-start(bf16[2,512,512]{2,1,0:T(8,128)(2,1)S(1)} %collective-permute-done), channel_id=1, source_target_pairs={{0,30},{2,0},{4,2},{6,4},{8,6},{10,8},{12,10},{14,12},{16,14},{18,... | collective-permute-start | bytes 3145736 | tf_op jit(solution)/shard_map/ppermute | solution.py:23
  79.4 15.8 %copy-start.7 = (bf16[2,512,512]{2,1,0:T(8,128)(2,1)}, bf16[2,512,512]{2,1,0:T(8,128)(2,1)S(1)}, u32[]{:S(2)}) copy-start(bf16[2,512,512]{2,1,0:T(8,128)(2,1)S(1)} %collective-permute-done.3) | copy-start | bytes 3145732
  79.4 19.4 %collective-permute-start.5 = (bf16[2,512,512]{2,1,0:T(8,128)(2,1)S(1)}, bf16[2,512,512]{2,1,0:T(8,128)(2,1)S(1)}, u32[]{:S(2)}, u32[]{:S(2)}) collective-permute-start(bf16[2,512,512]{2,1,0:T(8,128)(2,1)S(1)} %collective-permute-done.3), channel_id=1, source_target_pairs={{0,2},{2,4},{4,6},{6,8},{8,10},{10,12},{12,14},{14,16},{16,18},{18... | collective-permute-start | bytes 3145736 | tf_op jit(solution)/shard_map/ppermute | solution.py:21
  95.1 28.2 %copy-start.12 = (bf16[2,512,512]{2,1,0:T(8,128)(2,1)}, bf16[2,512,512]{2,1,0:T(8,128)(2,1)S(1)}, u32[]{:S(2)}) copy-start(bf16[2,512,512]{2,1,0:T(8,128)(2,1)S(1)} %collective-permute-done.2) | copy-start | bytes 3145732
  95.2 25.8 %collective-permute-start.4 = (bf16[2,512,512]{2,1,0:T(8,128)(2,1)S(1)}, bf16[2,512,512]{2,1,0:T(8,128)(2,1)}, u32[]{:S(2)}, u32[]{:S(2)}) collective-permute-start(bf16[2,512,512]{2,1,0:T(8,128)(2,1)S(1)} %collective-permute-done.2), channel_id=1, source_target_pairs={{0,30},{2,0},{4,2},{6,4},{8,6},{10,8},{12,10},{14,12},{16,14},{18,... | collective-permute-start | bytes 3145736 | tf_op jit(solution)/shard_map/ppermute | solution.py:23
  98.7 1.1 copy-start.9
  99.8 23.6 %collective-permute-start.7 = (bf16[2,512,512]{2,1,0:T(8,128)(2,1)S(1)}, bf16[2,512,512]{2,1,0:T(8,128)(2,1)}, u32[]{:S(2)}, u32[]{:S(2)}) collective-permute-start(bf16[2,512,512]{2,1,0:T(8,128)(2,1)S(1)} %collective-permute-done.5), channel_id=1, source_target_pairs={{0,2},{2,4},{4,6},{6,8},{8,10},{10,12},{12,14},{14,16},{16,18},{18... | collective-permute-start | bytes 3145736 | tf_op jit(solution)/shard_map/ppermute | solution.py:21
  120.9 31.9 %collective-permute-start.6 = (bf16[2,512,512]{2,1,0:T(8,128)(2,1)}, bf16[2,512,512]{2,1,0:T(8,128)(2,1)}, u32[]{:S(2)}, u32[]{:S(2)}) collective-permute-start(bf16[2,512,512]{2,1,0:T(8,128)(2,1)} %collective-permute-done.4), channel_id=1, source_target_pairs={{0,30},{2,0},{4,2},{6,4},{8,6},{10,8},{12,10},{14,12},{16,14},{18,... | collective-permute-start | bytes 3145736 | tf_op jit(solution)/shard_map/ppermute | solution.py:23
  123.4 30.0 %collective-permute-start.9 = (bf16[2,512,512]{2,1,0:T(8,128)(2,1)}, bf16[2,512,512]{2,1,0:T(8,128)(2,1)}, u32[]{:S(2)}, u32[]{:S(2)}) collective-permute-start(bf16[2,512,512]{2,1,0:T(8,128)(2,1)} %collective-permute-done.7), channel_id=1, source_target_pairs={{0,2},{2,4},{4,6},{6,8},{8,10},{10,12},{12,14},{14,16},{16,18},{18... | collective-permute-start | bytes 3145736 | tf_op jit(solution)/shard_map/ppermute | solution.py:21
  148.8 4.1 copy-start.5
  151.1 20.7 %copy-start.8 = (bf16[2,512,512]{2,1,0:T(8,128)(2,1)S(1)}, bf16[2,512,512]{2,1,0:T(8,128)(2,1)}, u32[]{:S(2)}) copy-start(bf16[2,512,512]{2,1,0:T(8,128)(2,1)} %copy-done.7) | copy-start | bytes 3145732
  151.1 21.0 %copy-start.13 = (bf16[2,512,512]{2,1,0:T(8,128)(2,1)S(1)}, bf16[2,512,512]{2,1,0:T(8,128)(2,1)}, u32[]{:S(2)}) copy-start(bf16[2,512,512]{2,1,0:T(8,128)(2,1)} %copy-done.12) | copy-start | bytes 3145732
  152.9 20.0 %collective-permute-start.8 = (bf16[2,512,512]{2,1,0:T(8,128)(2,1)}, bf16[2,512,512]{2,1,0:T(8,128)(2,1)S(1)}, u32[]{:S(2)}, u32[]{:S(2)}) collective-permute-start(bf16[2,512,512]{2,1,0:T(8,128)(2,1)} %collective-permute-done.6), channel_id=1, source_target_pairs={{0,30},{2,0},{4,2},{6,4},{8,6},{10,8},{12,10},{14,12},{16,14},{18,... | collective-permute-start | bytes 3145736 | tf_op jit(solution)/shard_map/ppermute | solution.py:23
  153.3 19.2 %copy-start.10 = (bf16[2,512,512]{2,1,0:T(8,128)(2,1)S(1)}, bf16[2,512,512]{2,1,0:T(8,128)(2,1)}, u32[]{:S(2)}) copy-start(bf16[2,512,512]{2,1,0:T(8,128)(2,1)} %copy-done.9) | copy-start | bytes 3145732
  153.3 21.2 %collective-permute-start.11 = (bf16[2,512,512]{2,1,0:T(8,128)(2,1)}, bf16[2,512,512]{2,1,0:T(8,128)(2,1)S(1)}, u32[]{:S(2)}, u32[]{:S(2)}) collective-permute-start(bf16[2,512,512]{2,1,0:T(8,128)(2,1)} %collective-permute-done.9), channel_id=1, source_target_pairs={{0,2},{2,4},{4,6},{6,8},{8,10},{10,12},{12,14},{14,16},{16,18},{18... | collective-permute-start | bytes 3145736 | tf_op jit(solution)/shard_map/ppermute | solution.py:21
  172.9 28.3 %collective-permute-start.10 = (bf16[2,512,512]{2,1,0:T(8,128)(2,1)S(1)}, bf16[2,512,512]{2,1,0:T(8,128)(2,1)S(1)}, u32[]{:S(2)}, u32[]{:S(2)}) collective-permute-start(bf16[2,512,512]{2,1,0:T(8,128)(2,1)S(1)} %collective-permute-done.8), channel_id=1, source_target_pairs={{0,30},{2,0},{4,2},{6,4},{8,6},{10,8},{12,10},{14,12},{16,14},{18,... | collective-permute-start | bytes 3145736 | tf_op jit(solution)/shard_map/ppermute | solution.py:23
  174.6 27.1 %collective-permute-start.13 = (bf16[2,512,512]{2,1,0:T(8,128)(2,1)S(1)}, bf16[2,512,512]{2,1,0:T(8,128)(2,1)S(1)}, u32[]{:S(2)}, u32[]{:S(2)}) collective-permute-start(bf16[2,512,512]{2,1,0:T(8,128)(2,1)S(1)} %collective-permute-done.11), channel_id=1, source_target_pairs={{0,2},{2,4},{4,6},{6,8},{8,10},{10,12},{12,14},{14,16},{16,18},{18... | collective-permute-start | bytes 3145736 | tf_op jit(solution)/shard_map/ppermute | solution.py:21
  201.2 21.7 %collective-permute-start.12 = (bf16[2,512,512]{2,1,0:T(8,128)(2,1)S(1)}, bf16[2,512,512]{2,1,0:T(8,128)(2,1)S(1)}, u32[]{:S(2)}, u32[]{:S(2)}) collective-permute-start(bf16[2,512,512]{2,1,0:T(8,128)(2,1)S(1)} %collective-permute-done.10), channel_id=1, source_target_pairs={{0,30},{2,0},{4,2},{6,4},{8,6},{10,8},{12,10},{14,12},{16,14},{18,... | collective-permute-start | bytes 3145736 | tf_op jit(solution)/shard_map/ppermute | solution.py:23
  201.7 22.3 %collective-permute-start.14 = (bf16[2,512,512]{2,1,0:T(8,128)(2,1)S(1)}, bf16[2,512,512]{2,1,0:T(8,128)(2,1)S(1)}, u32[]{:S(2)}, u32[]{:S(2)}) collective-permute-start(bf16[2,512,512]{2,1,0:T(8,128)(2,1)S(1)} %collective-permute-done.13), channel_id=1, source_target_pairs={{0,2},{2,4},{4,6},{6,8},{8,10},{10,12},{12,14},{14,16},{16,18},{18... | collective-permute-start | bytes 3145736 | tf_op jit(solution)/shard_map/ppermute | solution.py:21
  226.8 1.8 copy-start.16
  228.6 1.1 copy-start.15
  229.6 1.9 copy-start.18
  237.1 3.6 copy-start.14
  237.1 3.6 copy-start.19
  240.7 1.9 copy-start.3
  249.4 114.1 %all-to-all-start = ((bf16[192,16,512]{2,0,1:T(8,128)(2,1)}), bf16[192,16,512]{2,0,1:T(8,128)(2,1)S(1)}, u32[]{:S(2)}, u32[]{:S(2)}) async-start(bf16[192,16,512]{2,0,1:T(8,128)(2,1)} %bitcast.132), calls=%async_computation | async-start | bytes 6291456 | tf_op jit(solution)/shard_map/all_to_all | solution.py:112
  376.1 9.3 %copy-start.2 = (bf16[192,4,4,128]{3,2,1,0:T(4,128)(2,1)S(1)}, bf16[192,4,4,128]{3,2,1,0:T(4,128)(2,1)}, u32[]{:S(2)}) copy-start(bf16[192,4,4,128]{3,2,1,0:T(4,128)(2,1)} %copy.38) | copy-start | bytes 2359300
Sparse Core Ops, SparseCore 0:
  247.5 119.0 all-gather.1
